TPU v7x, 32 devices: a whole 2x2x4 slice. The times are simulated.
32 devices in a mesh: sector: 4 (over z), group: 8 (over y, x, core).
Axes of the slice: x: 2, y: 2, z: 4, core: 2. Of those that a mesh axis runs over, the one named last changes fastest.
Arguments:
- spectrum: float32 [1152, 128, 512], P('group', None, 'sector'), may hold values from 0.1 to 2
- land_mask: int32 [128, 512], P(None, 'sector'), may hold values 0 or 1
- wind_field: float32 [2, 128, 512], P(None, 'group', 'sector'), may hold values from -3 to 3
- assignment: int32 [1152], replicated, may hold values from 0 to 1151, each once
- courant: float32 [32], replicated, may hold values from 0.3 to 0.65
- growth: float32 [32], replicated, may hold values from 0.1 to 0.5
- whitecap: float32 [32], replicated, may hold values from 0.2 to 1
- weights: float32 [32], replicated, may hold values from 0.5 to 5
- spread: float32 [32, 36, 36], replicated, may hold values from -1 to 1
Outputs:
- updated: float32 [1152, 128, 512], P('group', None, 'sector')
Inputs may be any that keep to these rules, and one draw needn't show every extreme that they name: `assignment`: each component number appears exactly once.
All inputs are finite; a program needn't handle non-finite values. No bound on the sum of `land_mask` on one device may be relied on, other than what follows from the above.
Results may differ from a plain program's by a relative error of at most 0.00007.
Values sent between devices are 32-bit elements; how exact they have to be, the bound alone decides.
No kernel may reach another device: no remote copies, remote signals or barrier semaphores. Data moves between devices by JAX's collectives and lax.ppermute only.
A program may use at most 128 MiB of HBM per device.

v0:
```python
import math
import jax
import jax.numpy as jnp
from jax import lax
from jax.sharding import PartitionSpec as P

DIRS = 36
FREQ = 32
SUBSTEPS = 6
LAT = 128


def extended(cells, sides, width):
    for axis, dim in sides:
        count = lax.axis_size(axis)
        head = lax.slice_in_dim(cells, 0, width, axis=dim)
        tail = lax.slice_in_dim(cells, cells.shape[dim] - width, cells.shape[dim], axis=dim)
        cells = jnp.concatenate(
            [
                lax.ppermute(tail, axis, [(i, (i + 1) % count) for i in range(count)]),
                cells,
                lax.ppermute(head, axis, [((i + 1) % count, i) for i in range(count)]),
            ],
            axis=dim,
        )
    return cells


def freq_onehot(frequency):
    return (frequency[:, None] == jnp.arange(FREQ)[None, :]).astype(jnp.float32)


def flow_terms(kinds, courant):
    direction = kinds % DIRS
    frequency = kinds // DIRS
    angles = (direction.astype(jnp.float32) + 0.5) * (2.0 * math.pi / DIRS)
    speeds = jnp.dot(freq_onehot(frequency), courant, precision=lax.Precision.HIGHEST)
    latitude = (jnp.arange(LAT).astype(jnp.float32) + 0.5 - LAT / 2) * (math.pi / 2160.0)
    flow_x = speeds[:, None] * jnp.cos(angles)[:, None] / jnp.cos(latitude)[None, :]
    flow_y = speeds * jnp.sin(angles)
    return (flow_x, flow_y)


def combine(centre, from_west, from_east, rates):
    keep_rate, east_rate, west_rate, north_rate, south_rate = rates
    from_south = jnp.pad(centre[:, :-1], ((0, 0), (1, 0), (0, 0)))
    from_north = jnp.pad(centre[:, 1:], ((0, 0), (0, 1), (0, 0)))
    return (
        keep_rate * centre
        + east_rate * from_west
        + west_rate * from_east
        + north_rate * from_south
        + south_rate * from_north
    )


def propagate(wave, flow_x, flow_y, sea_mask):
    rates = (
        1.0 - jnp.abs(flow_x)[:, :, None] - jnp.abs(flow_y)[:, None, None],
        jnp.maximum(flow_x, 0.0)[:, :, None],
        jnp.maximum(-flow_x, 0.0)[:, :, None],
        jnp.maximum(flow_y, 0.0)[:, None, None],
        jnp.maximum(-flow_y, 0.0)[:, None, None],
    )
    for substep in range(SUBSTEPS):
        padded = extended(wave, (("sector", 2),), 1)
        wave = combine(wave, padded[:, :, :-2], padded[:, :, 2:], rates) * sea_mask[None]
    return wave


def local(spectrum, land_mask, wind_field, assignment, courant, growth, whitecap, weights, spread):
    member = lax.axis_index("group")
    comps_dev = spectrum.shape[0]
    lon_local = spectrum.shape[2]
    all_comps = assignment.shape[0]
    rows_dev = wind_field.shape[1]
    sea_mask = land_mask.astype(jnp.float32)
    kinds = lax.dynamic_slice_in_dim(assignment, member * comps_dev, comps_dev, 0)
    flow_x, flow_y = flow_terms(kinds, courant)
    moved = lax.all_to_all(
        propagate(spectrum, flow_x, flow_y, sea_mask),
        "group",
        split_axis=1,
        concat_axis=0,
        tiled=True,
    )
    points = rows_dev * lon_local
    energy = moved.reshape(all_comps, points)
    sea_rows = lax.dynamic_slice_in_dim(sea_mask, member * rows_dev, rows_dev, 0).reshape(points)
    winds = wind_field.reshape(2, points)
    direction = assignment % DIRS
    frequency = assignment // DIRS
    angles = (direction.astype(jnp.float32) + 0.5) * (2.0 * math.pi / DIRS)
    per_freq = jnp.stack((growth, whitecap, weights), axis=1)
    picked = jnp.dot(freq_onehot(frequency), per_freq, precision=lax.Precision.HIGHEST)
    kind_onehot = (assignment[:, None] == jnp.arange(all_comps)[None, :]).astype(jnp.float32)
    picked_rows = jnp.dot(
        kind_onehot, spread.reshape(FREQ * DIRS, DIRS), precision=lax.Precision.HIGHEST
    )
    dir_onehot = (jnp.arange(DIRS)[:, None] == direction[None, :]).astype(jnp.float32)
    same_freq = (frequency[:, None] == frequency[None, :]).astype(jnp.float32)
    coupling = jnp.dot(picked_rows, dir_onehot, precision=lax.Precision.HIGHEST) * same_freq
    loading = jnp.sum(picked[:, 2][:, None] * energy, axis=0) / all_comps
    drive = (
        jnp.cos(angles)[:, None] * winds[0][None, :] + jnp.sin(angles)[:, None] * winds[1][None, :]
    )
    exponent = (
        picked[:, 0][:, None] * jnp.maximum(drive, 0.0)
        - picked[:, 1][:, None] * (loading / (1.0 + loading))[None, :]
    )
    mixed = jnp.dot(coupling, energy, precision=lax.Precision.HIGHEST)
    renewed = (energy * jnp.exp(exponent) + 0.5 * mixed) * sea_rows[None, :]
    return lax.all_to_all(
        renewed.reshape(all_comps, rows_dev, lon_local),
        "group",
        split_axis=0,
        concat_axis=1,
        tiled=True,
    )


def solution(mesh):
    in_specs = (
        P("group", None, "sector"),
        P(None, "sector"),
        P(None, "group", "sector"),
        P(),
        P(),
        P(),
        P(),
        P(),
        P(),
    )
    out_specs = P("group", None, "sector")
    return jax.shard_map(local, mesh=mesh, in_specs=in_specs, out_specs=out_specs, check_vma=False)
```

profile of v0, /device:TPU:0, one launch (start us, length us, event | category | flops | bytes accessed | tf_op | source)
XLA Modules:
  0.0 494.8 jit_solution(8796984362894581755)
XLA Ops:
  0.0 9.6 %copy.15 = f32[144,128,128]{1,0,2:T(8,128)} copy(f32[144,128,128]{2,1,0:T(8,128)} %param.9) | data formatting | bytes 18874368 | tf_op args[0]
  9.6 0.9 fusion.83
  10.5 3.1 collective-permute-start
  13.6 2.1 collective-permute-start.1
  15.8 14.2 %fusion.82 = (f32[144,127,128]{1,0,2:T(8,128)}, f32[144,127,128]{1,0,2:T(8,128)}) fusion(f32[144,128,128]{1,0,2:T(8,128)} %copy.15), kind=kLoop, calls=%fused_computation.122 | loop fusion | bytes 37453824 | tf_op jit(solution)/shard_map/slice | solution.py:46
  30.8 16.4 %fusion.43 = f32[144,128,128]{1,0,2:T(8,128)S(1)} fusion(f32[144,128,1]{1,0,2:T(8,128)S(1)} %collective-permute-done.1, f32[144,128,128]{1,0,2:T(8,128)} %copy.15, f32[144,128,1]{1,0,2:T(8,128)S(1)} %collective-permute-done, f32[144,127,128]{1,0,2:T(8,128)} %get-tuple-element.31, f32[144,127,128]{1,0,2:T(8,128)} %get-tuple-element.30, ...), kind=kLoop, calls=%fused_computation.57 | loop fusion | flops 28311552 | bytes 38036608 | tf_op jit(solution)/shard_map/mul | solution.py:67
  47.3 3.8 collective-permute-start.3
  51.1 8.1 %fusion.80 = (f32[144,127,128]{1,0,2:T(8,128)}, f32[144,127,128]{1,0,2:T(8,128)}) fusion(f32[144,128,128]{1,0,2:T(8,128)S(1)} %fusion.43), kind=kLoop, calls=%fused_computation.120 | loop fusion | bytes 37453824 | tf_op jit(solution)/shard_map/slice | solution.py:46
  59.2 13.2 %fusion.36 = f32[144,128,128]{1,0,2:T(8,128)} fusion(f32[144,128,1]{1,0,2:T(8,128)S(1)} %collective-permute-done.3, f32[144,128,128]{1,0,2:T(8,128)S(1)} %fusion.43, f32[144,128,1]{1,0,2:T(8,128)S(1)} %collective-permute-done.2, f32[144,127,128]{1,0,2:T(8,128)} %get-tuple-element.27, f32[144,127,128]{1,0,2:T(8,128)} %get-tuple-element.26, ...), kind=kLoop, calls=%fused_computation.48 | loop fusion | flops 28311552 | bytes 38036608 | tf_op jit(solution)/shard_map/mul | solution.py:67
  73.4 3.8 collective-permute-start.5
  77.2 14.4 %fusion.78 = (f32[144,127,128]{1,0,2:T(8,128)}, f32[144,127,128]{1,0,2:T(8,128)}) fusion(f32[144,128,128]{1,0,2:T(8,128)} %fusion.36), kind=kLoop, calls=%fused_computation.118 | loop fusion | bytes 37453824 | tf_op jit(solution)/shard_map/slice | solution.py:46
  91.7 13.2 %fusion.29 = f32[144,128,128]{1,0,2:T(8,128)} fusion(f32[144,128,1]{1,0,2:T(8,128)S(1)} %collective-permute-done.5, f32[144,128,128]{1,0,2:T(8,128)S(1)} %bitcast.47, f32[144,128,1]{1,0,2:T(8,128)S(1)} %collective-permute-done.4, f32[144,127,128]{1,0,2:T(8,128)} %get-tuple-element.23, f32[144,127,128]{1,0,2:T(8,128)} %get-tuple-element.22, ...), kind=kLoop, calls=%fused_computation.39 | loop fusion | flops 28311552 | bytes 38036608 | tf_op jit(solution)/shard_map/mul | solution.py:67
  105.9 3.9 collective-permute-start.7
  109.9 14.4 %fusion.76 = (f32[144,127,128]{1,0,2:T(8,128)}, f32[144,127,128]{1,0,2:T(8,128)}) fusion(f32[144,128,128]{1,0,2:T(8,128)} %fusion.29), kind=kLoop, calls=%fused_computation.116 | loop fusion | bytes 37453824 | tf_op jit(solution)/shard_map/slice | solution.py:46
  124.3 13.2 %fusion.22 = f32[144,128,128]{1,0,2:T(8,128)} fusion(f32[144,128,1]{1,0,2:T(8,128)S(1)} %collective-permute-done.7, f32[144,128,128]{1,0,2:T(8,128)S(1)} %bitcast.49, f32[144,128,1]{1,0,2:T(8,128)S(1)} %collective-permute-done.6, f32[144,127,128]{1,0,2:T(8,128)} %get-tuple-element.19, f32[144,127,128]{1,0,2:T(8,128)} %get-tuple-element.18, ...), kind=kLoop, calls=%fused_computation.30 | loop fusion | flops 28311552 | bytes 38036608 | tf_op jit(solution)/shard_map/mul | solution.py:67
  138.5 3.8 collective-permute-start.9
  142.3 14.4 %fusion.74 = (f32[144,127,128]{1,0,2:T(8,128)}, f32[144,127,128]{1,0,2:T(8,128)}) fusion(f32[144,128,128]{1,0,2:T(8,128)} %fusion.22), kind=kLoop, calls=%fused_computation.114 | loop fusion | bytes 37453824 | tf_op jit(solution)/shard_map/slice | solution.py:46
  156.8 16.4 %fusion.15 = f32[144,128,128]{1,0,2:T(8,128)S(1)} fusion(f32[144,128,1]{1,0,2:T(8,128)S(1)} %collective-permute-done.9, f32[144,128,128]{1,0,2:T(8,128)} %fusion.22, f32[144,128,1]{1,0,2:T(8,128)S(1)} %collective-permute-done.8, f32[144,127,128]{1,0,2:T(8,128)} %get-tuple-element.15, f32[144,127,128]{1,0,2:T(8,128)} %get-tuple-element.14, ...), kind=kLoop, calls=%fused_computation.21 | loop fusion | flops 28311552 | bytes 38036608 | tf_op jit(solution)/shard_map/mul | solution.py:67
  173.2 3.8 collective-permute-start.11
  177.1 8.1 %fusion.72 = (f32[144,127,128]{1,0,2:T(8,128)}, f32[144,127,128]{1,0,2:T(8,128)}) fusion(f32[144,128,128]{1,0,2:T(8,128)S(1)} %fusion.15), kind=kLoop, calls=%fused_computation.112 | loop fusion | bytes 37453824 | tf_op jit(solution)/shard_map/slice | solution.py:46
  185.2 13.1 %fusion.8 = f32[144,128,128]{1,0,2:T(8,128)} fusion(f32[144,128,1]{1,0,2:T(8,128)S(1)} %collective-permute-done.11, f32[144,128,128]{1,0,2:T(8,128)S(1)} %fusion.15, f32[144,128,1]{1,0,2:T(8,128)S(1)} %collective-permute-done.10, f32[144,127,128]{1,0,2:T(8,128)} %get-tuple-element.11, f32[144,127,128]{1,0,2:T(8,128)} %get-tuple-element.10, ...), kind=kLoop, calls=%fused_computation.12 | loop fusion | flops 28311552 | bytes 38036608 | tf_op jit(solution)/shard_map/mul | solution.py:67
  198.3 9.6 %copy.23 = f32[144,128,128]{2,0,1:T(8,128)} copy(f32[144,128,128]{1,0,2:T(8,128)} %fusion.8) | data formatting | bytes 18874368 | tf_op jit(solution)/shard_map/mul | solution.py:67
  207.9 5.6 %all-to-all-start = ((f32[144,128,128]{2,0,1:T(8,128)}), f32[144,128,128]{2,0,1:T(8,128)}, u32[]{:S(2)}, u32[]{:S(2)}) async-start(f32[144,128,128]{2,0,1:T(8,128)} %copy.23), calls=%async_computation | async-start | bytes 18874368 | tf_op jit(solution)/shard_map/all_to_all | solution.py:80
  215.5 2.7 fusion.50
  218.2 4.8 convolution_select_fusion
  223.0 95.8 %all-to-all-done = f32[144,128,128]{2,0,1:T(8,128)} async-done(((f32[144,128,128]{2,0,1:T(8,128)}), f32[144,128,128]{2,0,1:T(8,128)}, u32[]{:S(2)}, u32[]{:S(2)}) %all-to-all-start) | async-done | bytes 9437216 | tf_op jit(solution)/shard_map/all_to_all | solution.py:80
  318.8 6.5 %copy.24 = f32[144,8,16,128]{3,2,0,1:T(8,128)S(1)} copy(f32[144,8,16,128]{3,0,2,1:T(8,128)} %bitcast.2) | data formatting | bytes 18874368 | tf_op jit(solution)/shard_map/all_to_all | solution.py:80
  325.3 7.5 %fusion.46 = f32[16,128]{1,0:T(8,128)S(1)} fusion(f32[8,144]{1,0:T(8,128)S(1)} %mul.415, f32[144,8,16,128]{3,0,2,1:T(8,128)} %bitcast.2), kind=kLoop, calls=%fused_computation.62 | loop fusion | flops 4716544 | bytes 9449984 | tf_op jit(solution)/shard_map/reduce_sum | solution.py:103
  332.9 46.4 %fusion.3 = f32[144,8,16,128]{3,1,2,0:T(8,128)S(1)} fusion(f32[1152,1152]{1,0:T(8,128)} %convolution_select_fusion, f32[144,8,16,128]{3,2,1,0:T(8,128)S(1)} %bitcast.52, f32[2048]{0:T(1024)S(1)} %dynamic-slice_bitcast_fusion, f32[2048]{0:T(1024)S(1)} %add_divide_fusion, f32[1152]{0:T(1024)S(1)} %get-tuple-element.7, f32[2048]{0:T(1024)S(1)} %get-tuple-element.35, ...), kind=kOutput, calls=%fused_computation.6 | convolution fusion | flops 32640860160 | bytes 24233984 | tf_op jit(solution)/shard_map/dot_general | solution.py:111
  379.3 2.3 copy.28
  381.5 107.8 %all_to_all.33 = f32[1152,16,128]{2,1,0:T(8,128)S(1)} all-to-all(f32[1152,16,128]{2,1,0:T(8,128)S(1)} %bitcast.50), channel_id=1, replica_groups=mesh['sector'=4,'group'=8] {'group'}, dimensions={0} | all-to-all | bytes 18874368 | tf_op jit(solution)/shard_map/all_to_all | solution.py:113
  489.3 5.2 %copy.26 = f32[8,144,16,128]{3,2,0,1:T(8,128)} copy(f32[8,144,16,128]{3,2,1,0:T(8,128)S(1)} %bitcast.51) | data formatting | bytes 18874368 | tf_op jit(solution)/shard_map/all_to_all | solution.py:113
  (72 shorter events, 5.8 us)
Async XLA Ops:
  0.0 30.1 %copy-start = (f32[32]{0:T(128)S(1)}, f32[32]{0:T(128)}, u32[]{:S(2)}) copy-start(f32[32]{0:T(128)} %param.13) | copy-start | bytes 388
  10.5 20.3 %collective-permute-start = (f32[144,128,1]{1,0,2:T(8,128)S(1)}, f32[144,128,1]{1,0,2:T(8,128)S(1)}, u32[]{:S(2)}, u32[]{:S(2)}) collective-permute-start(f32[144,128,1]{1,0,2:T(8,128)S(1)} %get-tuple-element.32), channel_id=1, source_target_pairs={{0,8},{8,16},{16,24},{24,0},{1,9},{9,17},{17,25},{25,1},{2,10},{10... | collective-permute-start | bytes 221192 | tf_op jit(solution)/shard_map/ppermute | solution.py:20
  13.6 17.2 %collective-permute-start.1 = (f32[144,128,1]{1,0,2:T(8,128)S(1)}, f32[144,128,1]{1,0,2:T(8,128)S(1)}, u32[]{:S(2)}, u32[]{:S(2)}) collective-permute-start(f32[144,128,1]{1,0,2:T(8,128)S(1)} %get-tuple-element.33), channel_id=1, source_target_pairs={{8,0},{16,8},{24,16},{0,24},{9,1},{17,9},{25,17},{1,25},{10,2},{18... | collective-permute-start | bytes 221192 | tf_op jit(solution)/shard_map/ppermute | solution.py:22
  15.8 14.3 %copy-start.4 = (s32[1152]{0:T(1024)S(1)}, s32[1152]{0:T(1024)}, u32[]{:S(2)}) copy-start(s32[1152]{0:T(1024)} %param.12) | copy-start | bytes 13828
  15.8 14.9 %copy-start.3 = (s32[128,128]{1,0:T(8,128)S(1)}, s32[128,128]{1,0:T(8,128)}, u32[]{:S(2)}) copy-start(s32[128,128]{1,0:T(8,128)} %param.10) | copy-start | bytes 196612
  47.2 12.0 %collective-permute-start.2 = (f32[144,128,1]{1,0,2:T(8,128)S(1)}, f32[144,128,1]{1,0,2:T(8,128)S(1)}, u32[]{:S(2)}, u32[]{:S(2)}) collective-permute-start(f32[144,128,1]{1,0,2:T(8,128)S(1)} %get-tuple-element.28), channel_id=1, source_target_pairs={{0,8},{8,16},{16,24},{24,0},{1,9},{9,17},{17,25},{25,1},{2,10},{10... | collective-permute-start | bytes 221192 | tf_op jit(solution)/shard_map/ppermute | solution.py:20
  47.3 11.9 %collective-permute-start.3 = (f32[144,128,1]{1,0,2:T(8,128)S(1)}, f32[144,128,1]{1,0,2:T(8,128)S(1)}, u32[]{:S(2)}, u32[]{:S(2)}) collective-permute-start(f32[144,128,1]{1,0,2:T(8,128)S(1)} %get-tuple-element.29), channel_id=1, source_target_pairs={{8,0},{16,8},{24,16},{0,24},{9,1},{17,9},{25,17},{1,25},{10,2},{18... | collective-permute-start | bytes 221192 | tf_op jit(solution)/shard_map/ppermute | solution.py:22
  73.3 18.3 %collective-permute-start.4 = (f32[144,128,1]{1,0,2:T(8,128)S(1)}, f32[144,128,1]{1,0,2:T(8,128)S(1)}, u32[]{:S(2)}, u32[]{:S(2)}) collective-permute-start(f32[144,128,1]{1,0,2:T(8,128)S(1)} %get-tuple-element.24), channel_id=1, source_target_pairs={{0,8},{8,16},{16,24},{24,0},{1,9},{9,17},{17,25},{25,1},{2,10},{10... | collective-permute-start | bytes 221192 | tf_op jit(solution)/shard_map/ppermute | solution.py:20
  73.4 18.2 %slice-start = ((s8[9437184]{0:T(1024)(128)(4,1)}), s8[4194304]{0:T(1024)(128)(4,1)S(1)}, s32[]{:S(2)}) async-start(s8[9437184]{0:T(1024)(128)(4,1)} %bitcast.46), calls=%async_computation.2 | async-start | bytes 8388608
  73.4 18.2 %slice-start.1 = ((s8[9437184]{0:T(1024)(128)(4,1)}), s8[4194304]{0:T(1024)(128)(4,1)S(1)}, s32[]{:S(2)}) async-start(s8[9437184]{0:T(1024)(128)(4,1)} %bitcast.46), calls=%async_computation.3 | async-start | bytes 8388608
  73.4 18.2 %slice-start.2 = ((s8[9437184]{0:T(1024)(128)(4,1)}), s8[1048576]{0:T(1024)(128)(4,1)S(1)}, s32[]{:S(2)}) async-start(s8[9437184]{0:T(1024)(128)(4,1)} %bitcast.46), calls=%async_computation.4 | async-start | bytes 2097152
  73.4 18.2 %collective-permute-start.5 = (f32[144,128,1]{1,0,2:T(8,128)S(1)}, f32[144,128,1]{1,0,2:T(8,128)S(1)}, u32[]{:S(2)}, u32[]{:S(2)}) collective-permute-start(f32[144,128,1]{1,0,2:T(8,128)S(1)} %get-tuple-element.25), channel_id=1, source_target_pairs={{8,0},{16,8},{24,16},{0,24},{9,1},{17,9},{25,17},{1,25},{10,2},{18... | collective-permute-start | bytes 221192 | tf_op jit(solution)/shard_map/ppermute | solution.py:22
  105.8 18.5 %collective-permute-start.6 = (f32[144,128,1]{1,0,2:T(8,128)S(1)}, f32[144,128,1]{1,0,2:T(8,128)S(1)}, u32[]{:S(2)}, u32[]{:S(2)}) collective-permute-start(f32[144,128,1]{1,0,2:T(8,128)S(1)} %get-tuple-element.20), channel_id=1, source_target_pairs={{0,8},{8,16},{16,24},{24,0},{1,9},{9,17},{17,25},{25,1},{2,10},{10... | collective-permute-start | bytes 221192 | tf_op jit(solution)/shard_map/ppermute | solution.py:20
  105.9 18.4 %slice-start.3 = ((s8[9437184]{0:T(1024)(128)(4,1)}), s8[4194304]{0:T(1024)(128)(4,1)S(1)}, s32[]{:S(2)}) async-start(s8[9437184]{0:T(1024)(128)(4,1)} %bitcast.48), calls=%async_computation.5 | async-start | bytes 8388608
  105.9 18.4 %slice-start.4 = ((s8[9437184]{0:T(1024)(128)(4,1)}), s8[4194304]{0:T(1024)(128)(4,1)S(1)}, s32[]{:S(2)}) async-start(s8[9437184]{0:T(1024)(128)(4,1)} %bitcast.48), calls=%async_computation.6 | async-start | bytes 8388608
  105.9 18.4 %slice-start.5 = ((s8[9437184]{0:T(1024)(128)(4,1)}), s8[1048576]{0:T(1024)(128)(4,1)S(1)}, s32[]{:S(2)}) async-start(s8[9437184]{0:T(1024)(128)(4,1)} %bitcast.48), calls=%async_computation.7 | async-start | bytes 2097152
  105.9 18.4 %collective-permute-start.7 = (f32[144,128,1]{1,0,2:T(8,128)S(1)}, f32[144,128,1]{1,0,2:T(8,128)S(1)}, u32[]{:S(2)}, u32[]{:S(2)}) collective-permute-start(f32[144,128,1]{1,0,2:T(8,128)S(1)} %get-tuple-element.21), channel_id=1, source_target_pairs={{8,0},{16,8},{24,16},{0,24},{9,1},{17,9},{25,17},{1,25},{10,2},{18... | collective-permute-start | bytes 221192 | tf_op jit(solution)/shard_map/ppermute | solution.py:22
  138.5 18.3 %collective-permute-start.8 = (f32[144,128,1]{1,0,2:T(8,128)S(1)}, f32[144,128,1]{1,0,2:T(8,128)S(1)}, u32[]{:S(2)}, u32[]{:S(2)}) collective-permute-start(f32[144,128,1]{1,0,2:T(8,128)S(1)} %get-tuple-element.16), channel_id=1, source_target_pairs={{0,8},{8,16},{16,24},{24,0},{1,9},{9,17},{17,25},{25,1},{2,10},{10... | collective-permute-start | bytes 221192 | tf_op jit(solution)/shard_map/ppermute | solution.py:20
  138.5 18.2 %collective-permute-start.9 = (f32[144,128,1]{1,0,2:T(8,128)S(1)}, f32[144,128,1]{1,0,2:T(8,128)S(1)}, u32[]{:S(2)}, u32[]{:S(2)}) collective-permute-start(f32[144,128,1]{1,0,2:T(8,128)S(1)} %get-tuple-element.17), channel_id=1, source_target_pairs={{8,0},{16,8},{24,16},{0,24},{9,1},{17,9},{25,17},{1,25},{10,2},{18... | collective-permute-start | bytes 221192 | tf_op jit(solution)/shard_map/ppermute | solution.py:22
  173.2 12.0 %collective-permute-start.10 = (f32[144,128,1]{1,0,2:T(8,128)S(1)}, f32[144,128,1]{1,0,2:T(8,128)S(1)}, u32[]{:S(2)}, u32[]{:S(2)}) collective-permute-start(f32[144,128,1]{1,0,2:T(8,128)S(1)} %get-tuple-element.12), channel_id=1, source_target_pairs={{0,8},{8,16},{16,24},{24,0},{1,9},{9,17},{17,25},{25,1},{2,10},{10... | collective-permute-start | bytes 221192 | tf_op jit(solution)/shard_map/ppermute | solution.py:20
  173.2 11.9 %collective-permute-start.11 = (f32[144,128,1]{1,0,2:T(8,128)S(1)}, f32[144,128,1]{1,0,2:T(8,128)S(1)}, u32[]{:S(2)}, u32[]{:S(2)}) collective-permute-start(f32[144,128,1]{1,0,2:T(8,128)S(1)} %get-tuple-element.13), channel_id=1, source_target_pairs={{8,0},{16,8},{24,16},{0,24},{9,1},{17,9},{25,17},{1,25},{10,2},{18... | collective-permute-start | bytes 221192 | tf_op jit(solution)/shard_map/ppermute | solution.py:22
  207.9 5.7 %copy-start.6 = (f32[32]{0:T(128)S(1)}, f32[32]{0:T(128)}, u32[]{:S(2)}) copy-start(f32[32]{0:T(128)} %param.16) | copy-start | bytes 388
  207.9 5.7 %copy-start.7 = (f32[32]{0:T(128)S(1)}, f32[32]{0:T(128)}, u32[]{:S(2)}) copy-start(f32[32]{0:T(128)} %param.15) | copy-start | bytes 388
  207.9 5.7 %copy-start.8 = (f32[32]{0:T(128)S(1)}, f32[32]{0:T(128)}, u32[]{:S(2)}) copy-start(f32[32]{0:T(128)} %param.14) | copy-start | bytes 388
  207.9 6.3 %copy-start.2 = (f32[32,36,36]{2,0,1:T(8,128)S(1)}, f32[32,36,36]{2,0,1:T(8,128)}, u32[]{:S(2)}) copy-start(f32[32,36,36]{2,0,1:T(8,128)} %param.17) | copy-start | bytes 497668
  207.9 7.5 %copy-start.5 = (f32[2,16,128]{2,1,0:T(8,128)S(1)}, f32[2,16,128]{2,1,0:T(8,128)}, u32[]{:S(2)}) copy-start(f32[2,16,128]{2,1,0:T(8,128)} %param.11) | copy-start | bytes 49156
  207.9 110.9 %all-to-all-start = ((f32[144,128,128]{2,0,1:T(8,128)}), f32[144,128,128]{2,0,1:T(8,128)}, u32[]{:S(2)}, u32[]{:S(2)}) async-start(f32[144,128,128]{2,0,1:T(8,128)} %copy.23), calls=%async_computation | async-start | bytes 18874368 | tf_op jit(solution)/shard_map/all_to_all | solution.py:80
  489.3 5.2 %copy-start.1 = (f32[32]{0:T(128)S(1)}, f32[32]{0:T(128)}, u32[]{:S(2)}) copy-start(f32[32]{0:T(128)} %param.13) | copy-start | bytes 388
where the time goes:
time: 503 us; the launch traced here: 495 us
  local copies, waits for them, and re-layouts  112 us (22%)
  blocking collectives  108 us (21%)
  waiting for transfers between devices  95.8 us (19%)
  other arithmetic  93.6 us (19%)
  matrix products  54.6 us (11%)
  starting transfers between devices  30.3 us (6%)
    all_to_all x1, blocking collectives, local(): lax.all_to_all(renewed.reshape(all_comps, rows_dev, lon_local), 'group',...  108 us
    all_to_all x1, waiting for transfers between devices, local(): lax.all_to_all(propagate(spectrum, flow_x, flow_y, sea_mask), 'group', sp...  95.8 us
    mul x6, other arithmetic, propagate(): combine(wave, padded[:, :, :-2], padded[:, :, 2:], rates) * sea_mask[None]  85.5 us
    slice x6, local copies, waits for them, and re-layouts, combine(): from_south = jnp.pad(centre[:, :-1], ((0, 0), (1, 0), (0, 0)))  73.7 us
    dot_general x1, matrix products, local(): mixed = jnp.dot(coupling, energy, precision=lax.Precision.HIGHEST)  46.4 us
    ppermute x6, starting transfers between devices, extended(): lax.ppermute(head, axis, [((i + 1) % count, i) for i in range(count)])  21.2 us
    unnamed x33, local copies, waits for them, and re-layouts  12.7 us
  transfers between devices with their start and end apart: 13, of which 1 were waited for; matrix products, arithmetic and copies ran while one was open for 17% of the time, Pallas kernels for 0%

commit v1 on v0

--- a/solution.py
+++ b/solution.py
@@ -8,6 +8,17 @@
 FREQ = 32
 SUBSTEPS = 6
 LAT = 128
+
+
+def cut_along(x, dim, count):
+    before, after = (x.shape[:dim], x.shape[dim + 1 :])
+    return jnp.moveaxis(x.reshape(*before, count, -1, *after), dim, 0)
+
+
+def joined_along(blocks, dim):
+    blocks = jnp.moveaxis(blocks, 0, dim)
+    shape = blocks.shape
+    return blocks.reshape(*shape[:dim], shape[dim] * shape[dim + 1], *shape[dim + 2 :])
 
 
 def extended(cells, sides, width):
@@ -77,13 +88,15 @@
     sea_mask = land_mask.astype(jnp.float32)
     kinds = lax.dynamic_slice_in_dim(assignment, member * comps_dev, comps_dev, 0)
     flow_x, flow_y = flow_terms(kinds, courant)
-    moved = lax.all_to_all(
-        propagate(spectrum, flow_x, flow_y, sea_mask),
-        "group",
-        split_axis=1,
-        concat_axis=0,
-        tiled=True,
-    )
+    value = propagate(spectrum, flow_x, flow_y, sea_mask)
+    peers, place = (lax.axis_size("group"), lax.axis_index("group"))
+    blocks = cut_along(value, 1, peers)
+    outs = [blocks[place]]
+    for step in range(1, peers):
+        sent = blocks[place ^ step]
+        outs.append(lax.ppermute(sent, "group", [(i_2, i_2 ^ step) for i_2 in range(peers)]))
+    blocks = jnp.stack(outs)[place ^ jnp.arange(peers)]
+    moved = joined_along(blocks, 0)
     points = rows_dev * lon_local
     energy = moved.reshape(all_comps, points)
     sea_rows = lax.dynamic_slice_in_dim(sea_mask, member * rows_dev, rows_dev, 0).reshape(points)

time: 503 us -> 807 us (1.60)
  local copies, waits for them, and re-layouts: 112 us -> 346 us
  other arithmetic: 93.6 us -> 172 us
    slice x6 -> x11, local copies, waits for them, and re-layouts: 3.74 us -> 118 us  [extended(): lax.slice_in_dim(cells, cells.shape[dim] - width, cells.shape[dim], axis=...]
    all_to_all x1 -> x0, waiting for transfers between devices: 95.8 us -> none  [local(): lax.all_to_all(propagate(spectrum, flow_x, flow_y, sea_mask), 'group', sp...]
    ppermute x0 -> x7, waiting for transfers between devices: none -> 89.8 us  [local(): lax.ppermute(sent, 'group', [(i_2, i_2 ^ step) for i_2 in range(peers)])]
    mul x6, other arithmetic: 85.5 us -> 165 us  [propagate(): combine(wave, padded[:, :, :-2], padded[:, :, 2:], rates) * sea_mask[None]]
    ppermute x0 -> x12, local copies, waits for them, and re-layouts: none -> 61.5 us  [the longest x6 31 us: extended(): lax.ppermute(tail, axis, [(i, (i + 1) % count) for i in range(count)])]
    slice x0 -> x5, local copies, waits for them, and re-layouts: none -> 29 us  [extended(): head = lax.slice_in_dim(cells, 0, width, axis=dim)]
    slice x6, local copies, waits for them, and re-layouts: 73.7 us -> 87.8 us  [combine(): from_south = jnp.pad(centre[:, :-1], ((0, 0), (1, 0), (0, 0)))]
    unnamed x33 -> x49, local copies, waits for them, and re-layouts: 12.7 us -> 24 us
  transfers between devices with their start and end apart: 13 -> 19, of which waited for: 1 -> 3; matrix products, arithmetic and copies ran while one was open for 17% -> 22% of each run, Pallas kernels for 0% -> 0%
where the time goes in v1:
time: 807 us; the launch traced here: 804 us
  local copies, waits for them, and re-layouts  346 us (43%)
  other arithmetic  172 us (21%)
  blocking collectives  109 us (14%)
  waiting for transfers between devices  89.8 us (11%)
  matrix products  52.3 us (6%)
  starting transfers between devices  33.3 us (4%)
    mul x6, other arithmetic, propagate(): combine(wave, padded[:, :, :-2], padded[:, :, 2:], rates) * sea_mask[None]  165 us
    slice x11, local copies, waits for them, and re-layouts, extended(): lax.slice_in_dim(cells, cells.shape[dim] - width, cells.shape[dim], axis=...  118 us
    all_to_all x1, blocking collectives, local(): lax.all_to_all(renewed.reshape(all_comps, rows_dev, lon_local), 'group',...  109 us
    ppermute x7, waiting for transfers between devices, local(): lax.ppermute(sent, 'group', [(i_2, i_2 ^ step) for i_2 in range(peers)])  89.8 us
    slice x6, local copies, waits for them, and re-layouts, combine(): from_south = jnp.pad(centre[:, :-1], ((0, 0), (1, 0), (0, 0)))  87.8 us
    dot_general x1, matrix products, local(): mixed = jnp.dot(coupling, energy, precision=lax.Precision.HIGHEST)  44.2 us
    ppermute x6, local copies, waits for them, and re-layouts, extended(): lax.ppermute(tail, axis, [(i, (i + 1) % count) for i in range(count)])  31 us
    ppermute x6, local copies, waits for them, and re-layouts, extended(): lax.ppermute(head, axis, [((i + 1) % count, i) for i in range(count)])  30.5 us
  transfers between devices with their start and end apart: 19, of which 3 were waited for; matrix products, arithmetic and copies ran while one was open for 22% of the time, Pallas kernels for 0%

profile of v1, /device:TPU:0, one launch (start us, length us, event | category | flops | bytes accessed | tf_op | source)
XLA Modules:
  0.0 803.9 jit_solution(11567643149918698903)
XLA Ops:
  0.0 14.8 %fusion.83 = (f32[144,128,1]{2,1,0:T(8,128)}, f32[144,128,1]{2,1,0:T(8,128)}) fusion(f32[144,128,128]{2,1,0:T(8,128)} %param.9), kind=kLoop, calls=%fused_computation.141 | loop fusion | bytes 294912 | tf_op jit(solution)/shard_map/slice | solution.py:28
  14.8 5.8 copy.49
  31.9 14.7 %fusion.82 = (f32[144,127,128]{2,1,0:T(8,128)}, f32[144,127,128]{2,1,0:T(8,128)}) fusion(f32[144,128,128]{2,1,0:T(8,128)} %param.9), kind=kLoop, calls=%fused_computation.140 | loop fusion | bytes 37453824 | tf_op jit(solution)/shard_map/slice | solution.py:57
  66.3 27.0 %fusion.43 = f32[144,128,128]{2,1,0:T(8,128)} fusion(f32[144,128,1]{2,1,0:T(8,128)} %copy.26, f32[144,128,128]{2,1,0:T(8,128)} %param.9, f32[144,128,1]{2,1,0:T(8,128)} %copy.24, f32[144,127,128]{2,1,0:T(8,128)} %get-tuple-element.38, f32[144,127,128]{2,1,0:T(8,128)} %get-tuple-element.37, f32[128,128]{1,0:T(8,128)S(1)} %convert_element_type.37, ...), kind=kLoop, calls=%fused_computation.58 | loop fusion | flops 28311552 | bytes 38036608 | tf_op jit(solution)/shard_map/mul | solution.py:78
  93.3 15.0 %fusion.81 = (f32[144,128,1]{2,1,0:T(8,128)}, f32[144,128,1]{2,1,0:T(8,128)}) fusion(f32[144,128,128]{2,1,0:T(8,128)} %fusion.43), kind=kLoop, calls=%fused_computation.139 | loop fusion | bytes 294912 | tf_op jit(solution)/shard_map/slice | solution.py:28
  114.1 5.8 copy.29
  124.0 14.7 %fusion.80 = (f32[144,127,128]{2,1,0:T(8,128)}, f32[144,127,128]{2,1,0:T(8,128)}) fusion(f32[144,128,128]{2,1,0:T(8,128)} %fusion.43), kind=kLoop, calls=%fused_computation.138 | loop fusion | bytes 37453824 | tf_op jit(solution)/shard_map/slice | solution.py:57
  148.9 27.9 %fusion.36 = f32[144,128,128]{2,1,0:T(8,128)} fusion(f32[144,128,1]{2,1,0:T(8,128)} %copy.30, f32[144,128,128]{2,1,0:T(8,128)} %fusion.43, f32[144,128,1]{2,1,0:T(8,128)} %copy.28, f32[144,127,128]{2,1,0:T(8,128)} %get-tuple-element.34, f32[144,127,128]{2,1,0:T(8,128)} %get-tuple-element.33, f32[128,128]{1,0:T(8,128)S(1)} %convert_element_type.37, ...), kind=kLoop, calls=%fused_computation.49 | loop fusion | flops 28311552 | bytes 38036608 | tf_op jit(solution)/shard_map/mul | solution.py:78
  176.8 14.8 %fusion.79 = (f32[144,128,1]{2,1,0:T(8,128)}, f32[144,128,1]{2,1,0:T(8,128)}) fusion(f32[144,128,128]{2,1,0:T(8,128)} %fusion.36), kind=kLoop, calls=%fused_computation.137 | loop fusion | bytes 294912 | tf_op jit(solution)/shard_map/slice | solution.py:28
  197.5 5.8 copy.33
  207.2 14.5 %fusion.78 = (f32[144,127,128]{2,1,0:T(8,128)}, f32[144,127,128]{2,1,0:T(8,128)}) fusion(f32[144,128,128]{2,1,0:T(8,128)} %fusion.36), kind=kLoop, calls=%fused_computation.136 | loop fusion | bytes 37453824 | tf_op jit(solution)/shard_map/slice | solution.py:57
  231.9 27.2 %fusion.29 = f32[144,128,128]{2,1,0:T(8,128)} fusion(f32[144,128,1]{2,1,0:T(8,128)} %copy.34, f32[144,128,128]{2,1,0:T(8,128)} %fusion.36, f32[144,128,1]{2,1,0:T(8,128)} %copy.32, f32[144,127,128]{2,1,0:T(8,128)} %get-tuple-element.30, f32[144,127,128]{2,1,0:T(8,128)} %get-tuple-element.29, f32[128,128]{1,0:T(8,128)S(1)} %convert_element_type.37, ...), kind=kLoop, calls=%fused_computation.40 | loop fusion | flops 28311552 | bytes 38036608 | tf_op jit(solution)/shard_map/mul | solution.py:78
  259.1 15.0 %fusion.77 = (f32[144,128,1]{2,1,0:T(8,128)}, f32[144,128,1]{2,1,0:T(8,128)}) fusion(f32[144,128,128]{2,1,0:T(8,128)} %fusion.29), kind=kLoop, calls=%fused_computation.135 | loop fusion | bytes 294912 | tf_op jit(solution)/shard_map/slice | solution.py:28
  279.9 5.8 copy.37
  290.0 14.7 %fusion.76 = (f32[144,127,128]{2,1,0:T(8,128)}, f32[144,127,128]{2,1,0:T(8,128)}) fusion(f32[144,128,128]{2,1,0:T(8,128)} %fusion.29), kind=kLoop, calls=%fused_computation.134 | loop fusion | bytes 37453824 | tf_op jit(solution)/shard_map/slice | solution.py:57
  314.9 27.9 %fusion.22 = f32[144,128,128]{2,1,0:T(8,128)} fusion(f32[144,128,1]{2,1,0:T(8,128)} %copy.38, f32[144,128,128]{2,1,0:T(8,128)} %fusion.29, f32[144,128,1]{2,1,0:T(8,128)} %copy.36, f32[144,127,128]{2,1,0:T(8,128)} %get-tuple-element.26, f32[144,127,128]{2,1,0:T(8,128)} %get-tuple-element.25, f32[128,128]{1,0:T(8,128)S(1)} %convert_element_type.37, ...), kind=kLoop, calls=%fused_computation.31 | loop fusion | flops 28311552 | bytes 38036608 | tf_op jit(solution)/shard_map/mul | solution.py:78
  342.8 14.8 %fusion.75 = (f32[144,128,1]{2,1,0:T(8,128)}, f32[144,128,1]{2,1,0:T(8,128)}) fusion(f32[144,128,128]{2,1,0:T(8,128)} %fusion.22), kind=kLoop, calls=%fused_computation.133 | loop fusion | bytes 294912 | tf_op jit(solution)/shard_map/slice | solution.py:28
  363.5 5.8 copy.41
  373.2 14.5 %fusion.74 = (f32[144,127,128]{2,1,0:T(8,128)}, f32[144,127,128]{2,1,0:T(8,128)}) fusion(f32[144,128,128]{2,1,0:T(8,128)} %fusion.22), kind=kLoop, calls=%fused_computation.132 | loop fusion | bytes 37453824 | tf_op jit(solution)/shard_map/slice | solution.py:57
  397.9 27.2 %fusion.15 = f32[144,128,128]{2,1,0:T(8,128)} fusion(f32[144,128,1]{2,1,0:T(8,128)} %copy.42, f32[144,128,128]{2,1,0:T(8,128)} %fusion.22, f32[144,128,1]{2,1,0:T(8,128)} %copy.40, f32[144,127,128]{2,1,0:T(8,128)} %get-tuple-element.22, f32[144,127,128]{2,1,0:T(8,128)} %get-tuple-element.21, f32[128,128]{1,0:T(8,128)S(1)} %convert_element_type.37, ...), kind=kLoop, calls=%fused_computation.22 | loop fusion | flops 28311552 | bytes 38036608 | tf_op jit(solution)/shard_map/mul | solution.py:78
  425.1 15.0 %fusion.73 = (f32[144,128,1]{2,1,0:T(8,128)}, f32[144,128,1]{2,1,0:T(8,128)}) fusion(f32[144,128,128]{2,1,0:T(8,128)} %fusion.15), kind=kLoop, calls=%fused_computation.131 | loop fusion | bytes 294912 | tf_op jit(solution)/shard_map/slice | solution.py:28
  445.9 5.8 copy.45
  455.8 14.7 %fusion.72 = (f32[144,127,128]{2,1,0:T(8,128)}, f32[144,127,128]{2,1,0:T(8,128)}) fusion(f32[144,128,128]{2,1,0:T(8,128)} %fusion.15), kind=kLoop, calls=%fused_computation.130 | loop fusion | bytes 37453824 | tf_op jit(solution)/shard_map/slice | solution.py:57
  480.7 27.9 %fusion.8 = f32[144,128,128]{2,1,0:T(8,128)} fusion(f32[144,128,1]{2,1,0:T(8,128)} %copy.46, f32[144,128,128]{2,1,0:T(8,128)} %fusion.15, f32[144,128,1]{2,1,0:T(8,128)} %copy.44, f32[144,127,128]{2,1,0:T(8,128)} %get-tuple-element.18, f32[144,127,128]{2,1,0:T(8,128)} %get-tuple-element.17, f32[128,128]{1,0:T(8,128)S(1)} %convert_element_type.37, ...), kind=kLoop, calls=%fused_computation.13 | loop fusion | flops 28311552 | bytes 38036608 | tf_op jit(solution)/shard_map/mul | solution.py:78
  508.6 6.8 dynamic-slice_bitcast_fusion
  530.2 15.5 %collective-permute-done.13 = f32[144,16,128]{2,1,0:T(8,128)S(1)} collective-permute-done((f32[144,16,128]{2,1,0:T(8,128)}, f32[144,16,128]{2,1,0:T(8,128)S(1)}, u32[]{:S(2)}, u32[]{:S(2)}) %collective-permute-start.13) | collective-permute-done | bytes 1179680 | tf_op jit(solution)/shard_map/ppermute | solution.py:97
  548.2 22.1 %collective-permute-done.14 = f32[144,16,128]{2,1,0:T(8,128)S(1)} collective-permute-done((f32[144,16,128]{2,1,0:T(8,128)}, f32[144,16,128]{2,1,0:T(8,128)S(1)}, u32[]{:S(2)}, u32[]{:S(2)}) %collective-permute-start.14) | collective-permute-done | bytes 1179680 | tf_op jit(solution)/shard_map/ppermute | solution.py:97
  572.4 52.2 %collective-permute-done.16 = f32[144,16,128]{2,1,0:T(8,128)S(1)} collective-permute-done((f32[144,16,128]{2,1,0:T(8,128)}, f32[144,16,128]{2,1,0:T(8,128)S(1)}, u32[]{:S(2)}, u32[]{:S(2)}) %collective-permute-start.16) | collective-permute-done | bytes 1179680 | tf_op jit(solution)/shard_map/ppermute | solution.py:97
  627.9 8.5 %gather_fusion = f32[8,144,16,128]{3,2,1,0:T(8,128)} fusion(f32[8,144,16,128]{3,2,1,0:T(8,128)} %bitcast_dynamic-update-slice_fusion, s32[1024]{0:T(1024)S(1)} %pad_clamp_fusion), kind=kCustom, calls=%fused_computation | custom fusion | bytes 18874400 | tf_op jit(solution)/shard_map/gather | solution.py:98
  636.5 5.9 multiply_reduce_fusion
  642.9 44.2 %fusion.3 = f32[144,8,16,128]{3,1,2,0:T(8,128)S(1)} fusion(f32[1152,1152]{1,0:T(8,128)} %convolution_select_fusion, f32[144,8,16,128]{3,2,1,0:T(8,128)S(1)} %bitcast.76, f32[2048]{0:T(1024)S(1)} %copy-done.14, f32[2048]{0:T(1024)S(1)} %add_divide_fusion, f32[1152]{0:T(1024)S(1)} %copy-done.11, f32[2048]{0:T(1024)S(1)} %copy-done.15, ...), kind=kOutput, calls=%fused_computation.7 | convolution fusion | flops 32640860160 | bytes 24233984 | tf_op jit(solution)/shard_map/dot_general | solution.py:124
  689.4 109.0 %all_to_all.18 = f32[1152,16,128]{2,1,0:T(8,128)S(1)} all-to-all(f32[1152,16,128]{2,1,0:T(8,128)S(1)} %bitcast.77), channel_id=1, replica_groups=mesh['sector'=4,'group'=8] {'group'}, dimensions={0} | all-to-all | bytes 18874368 | tf_op jit(solution)/shard_map/all_to_all | solution.py:126
  (122 shorter events, 161.9 us)
Async XLA Ops:
  0.0 46.8 %copy-start = (f32[32]{0:T(128)S(1)}, f32[32]{0:T(128)}, u32[]{:S(2)}) copy-start(f32[32]{0:T(128)} %param.13) | copy-start | bytes 388
  20.6 35.3 %collective-permute-start = (f32[144,128,1]{1,0,2:T(8,128)S(1)}, f32[144,128,1]{1,0,2:T(8,128)S(1)}, u32[]{:S(2)}, u32[]{:S(2)}) collective-permute-start(f32[144,128,1]{1,0,2:T(8,128)S(1)} %copy.49), channel_id=1, source_target_pairs={{0,8},{8,16},{16,24},{24,0},{1,9},{9,17},{17,25},{25,1},{2,10},{10... | collective-permute-start | bytes 221192 | tf_op jit(solution)/shard_map/ppermute | solution.py:31
  29.6 31.6 %collective-permute-start.1 = (f32[144,128,1]{1,0,2:T(8,128)S(1)}, f32[144,128,1]{1,0,2:T(8,128)S(1)}, u32[]{:S(2)}, u32[]{:S(2)}) collective-permute-start(f32[144,128,1]{1,0,2:T(8,128)S(1)} %copy.50), channel_id=1, source_target_pairs={{8,0},{16,8},{24,16},{0,24},{9,1},{17,9},{25,17},{1,25},{10,2},{18... | collective-permute-start | bytes 221192 | tf_op jit(solution)/shard_map/ppermute | solution.py:33
  31.9 14.8 %copy-start.7 = (s32[1152]{0:T(1024)S(1)}, s32[1152]{0:T(1024)}, u32[]{:S(2)}) copy-start(s32[1152]{0:T(1024)} %param.12) | copy-start | bytes 13828
  31.9 15.3 %copy-start.3 = (f32[32,36,36]{2,0,1:T(8,128)S(1)}, f32[32,36,36]{2,0,1:T(8,128)}, u32[]{:S(2)}) copy-start(f32[32,36,36]{2,0,1:T(8,128)} %param.17) | copy-start | bytes 497668
  46.6 9.3 %copy-start.6 = (s32[128,128]{1,0:T(8,128)S(1)}, s32[128,128]{1,0:T(8,128)}, u32[]{:S(2)}) copy-start(s32[128,128]{1,0:T(8,128)} %param.10) | copy-start | bytes 196612
  46.7 14.5 %copy-start.4 = (s32[1152]{0:T(1024)}, s32[1152]{0:T(1024)S(1)}, u32[]{:S(2)}) copy-start(s32[1152]{0:T(1024)S(1)} %get-tuple-element.46) | copy-start | bytes 13828
  114.1 24.6 %collective-permute-start.2 = (f32[144,128,1]{1,0,2:T(8,128)S(1)}, f32[144,128,1]{1,0,2:T(8,128)S(1)}, u32[]{:S(2)}, u32[]{:S(2)}) collective-permute-start(f32[144,128,1]{1,0,2:T(8,128)S(1)} %copy.27), channel_id=1, source_target_pairs={{0,8},{8,16},{16,24},{24,0},{1,9},{9,17},{17,25},{25,1},{2,10},{10... | collective-permute-start | bytes 221192 | tf_op jit(solution)/shard_map/ppermute | solution.py:31
  120.0 23.9 %collective-permute-start.3 = (f32[144,128,1]{1,0,2:T(8,128)S(1)}, f32[144,128,1]{1,0,2:T(8,128)S(1)}, u32[]{:S(2)}, u32[]{:S(2)}) collective-permute-start(f32[144,128,1]{1,0,2:T(8,128)S(1)} %copy.29), channel_id=1, source_target_pairs={{8,0},{16,8},{24,16},{0,24},{9,1},{17,9},{25,17},{1,25},{10,2},{18... | collective-permute-start | bytes 221192 | tf_op jit(solution)/shard_map/ppermute | solution.py:33
  197.4 24.3 %collective-permute-start.4 = (f32[144,128,1]{1,0,2:T(8,128)S(1)}, f32[144,128,1]{1,0,2:T(8,128)S(1)}, u32[]{:S(2)}, u32[]{:S(2)}) collective-permute-start(f32[144,128,1]{1,0,2:T(8,128)S(1)} %copy.31), channel_id=1, source_target_pairs={{0,8},{8,16},{16,24},{24,0},{1,9},{9,17},{17,25},{25,1},{2,10},{10... | collective-permute-start | bytes 221192 | tf_op jit(solution)/shard_map/ppermute | solution.py:31
  203.3 23.6 %collective-permute-start.5 = (f32[144,128,1]{1,0,2:T(8,128)S(1)}, f32[144,128,1]{1,0,2:T(8,128)S(1)}, u32[]{:S(2)}, u32[]{:S(2)}) collective-permute-start(f32[144,128,1]{1,0,2:T(8,128)S(1)} %copy.33), channel_id=1, source_target_pairs={{8,0},{16,8},{24,16},{0,24},{9,1},{17,9},{25,17},{1,25},{10,2},{18... | collective-permute-start | bytes 221192 | tf_op jit(solution)/shard_map/ppermute | solution.py:33
  279.9 24.8 %collective-permute-start.6 = (f32[144,128,1]{1,0,2:T(8,128)S(1)}, f32[144,128,1]{1,0,2:T(8,128)S(1)}, u32[]{:S(2)}, u32[]{:S(2)}) collective-permute-start(f32[144,128,1]{1,0,2:T(8,128)S(1)} %copy.35), channel_id=1, source_target_pairs={{0,8},{8,16},{16,24},{24,0},{1,9},{9,17},{17,25},{25,1},{2,10},{10... | collective-permute-start | bytes 221192 | tf_op jit(solution)/shard_map/ppermute | solution.py:31
  285.8 24.1 %collective-permute-start.7 = (f32[144,128,1]{1,0,2:T(8,128)S(1)}, f32[144,128,1]{1,0,2:T(8,128)S(1)}, u32[]{:S(2)}, u32[]{:S(2)}) collective-permute-start(f32[144,128,1]{1,0,2:T(8,128)S(1)} %copy.37), channel_id=1, source_target_pairs={{8,0},{16,8},{24,16},{0,24},{9,1},{17,9},{25,17},{1,25},{10,2},{18... | collective-permute-start | bytes 221192 | tf_op jit(solution)/shard_map/ppermute | solution.py:33
  363.4 24.3 %collective-permute-start.8 = (f32[144,128,1]{1,0,2:T(8,128)S(1)}, f32[144,128,1]{1,0,2:T(8,128)S(1)}, u32[]{:S(2)}, u32[]{:S(2)}) collective-permute-start(f32[144,128,1]{1,0,2:T(8,128)S(1)} %copy.39), channel_id=1, source_target_pairs={{0,8},{8,16},{16,24},{24,0},{1,9},{9,17},{17,25},{25,1},{2,10},{10... | collective-permute-start | bytes 221192 | tf_op jit(solution)/shard_map/ppermute | solution.py:31
  369.3 23.6 %collective-permute-start.9 = (f32[144,128,1]{1,0,2:T(8,128)S(1)}, f32[144,128,1]{1,0,2:T(8,128)S(1)}, u32[]{:S(2)}, u32[]{:S(2)}) collective-permute-start(f32[144,128,1]{1,0,2:T(8,128)S(1)} %copy.41), channel_id=1, source_target_pairs={{8,0},{16,8},{24,16},{0,24},{9,1},{17,9},{25,17},{1,25},{10,2},{18... | collective-permute-start | bytes 221192 | tf_op jit(solution)/shard_map/ppermute | solution.py:33
  445.9 24.6 %collective-permute-start.10 = (f32[144,128,1]{1,0,2:T(8,128)S(1)}, f32[144,128,1]{1,0,2:T(8,128)S(1)}, u32[]{:S(2)}, u32[]{:S(2)}) collective-permute-start(f32[144,128,1]{1,0,2:T(8,128)S(1)} %copy.43), channel_id=1, source_target_pairs={{0,8},{8,16},{16,24},{24,0},{1,9},{9,17},{17,25},{25,1},{2,10},{10... | collective-permute-start | bytes 221192 | tf_op jit(solution)/shard_map/ppermute | solution.py:31
  451.7 23.8 %collective-permute-start.11 = (f32[144,128,1]{1,0,2:T(8,128)S(1)}, f32[144,128,1]{1,0,2:T(8,128)S(1)}, u32[]{:S(2)}, u32[]{:S(2)}) collective-permute-start(f32[144,128,1]{1,0,2:T(8,128)S(1)} %copy.45), channel_id=1, source_target_pairs={{8,0},{16,8},{24,16},{0,24},{9,1},{17,9},{25,17},{1,25},{10,2},{18... | collective-permute-start | bytes 221192 | tf_op jit(solution)/shard_map/ppermute | solution.py:33
  508.6 7.5 copy-start.5
  508.6 7.5 copy-start.16
  508.6 7.4 copy-start.17
  508.6 7.4 copy-start.18
  508.6 11.8 %copy-start.8 = (s32[1152]{0:T(1024)S(1)}, s32[1152]{0:T(1024)}, u32[]{:S(2)}) copy-start(s32[1152]{0:T(1024)} %param.12) | copy-start | bytes 13828
  515.4 11.1 %collective-permute-start.12 = (f32[144,16,128]{2,1,0:T(8,128)}, f32[144,16,128]{2,1,0:T(8,128)S(1)}, u32[]{:S(2)}, u32[]{:S(2)}) collective-permute-start(f32[144,16,128]{2,1,0:T(8,128)} %get-tuple-element.16), channel_id=1, source_target_pairs={{0,1},{1,0},{2,3},{3,2},{4,5},{5,4},{6,7},{7,6},{8,9},{9,8},{10,11... | collective-permute-start | bytes 3538952 | tf_op jit(solution)/shard_map/ppermute | solution.py:97
  516.5 29.1 %collective-permute-start.13 = (f32[144,16,128]{2,1,0:T(8,128)}, f32[144,16,128]{2,1,0:T(8,128)S(1)}, u32[]{:S(2)}, u32[]{:S(2)}) collective-permute-start(f32[144,16,128]{2,1,0:T(8,128)} %get-tuple-element.15), channel_id=1, source_target_pairs={{0,2},{1,3},{2,0},{3,1},{4,6},{5,7},{6,4},{7,5},{8,10},{9,11},{10,... | collective-permute-start | bytes 3538952 | tf_op jit(solution)/shard_map/ppermute | solution.py:97
  518.9 51.3 %collective-permute-start.14 = (f32[144,16,128]{2,1,0:T(8,128)}, f32[144,16,128]{2,1,0:T(8,128)S(1)}, u32[]{:S(2)}, u32[]{:S(2)}) collective-permute-start(f32[144,16,128]{2,1,0:T(8,128)} %get-tuple-element.14), channel_id=1, source_target_pairs={{0,3},{1,2},{2,1},{3,0},{4,7},{5,6},{6,5},{7,4},{8,11},{9,10},{10,... | collective-permute-start | bytes 3538952 | tf_op jit(solution)/shard_map/ppermute | solution.py:97
  521.1 50.2 %collective-permute-start.15 = (f32[144,16,128]{2,1,0:T(8,128)}, f32[144,16,128]{2,1,0:T(8,128)S(1)}, u32[]{:S(2)}, u32[]{:S(2)}) collective-permute-start(f32[144,16,128]{2,1,0:T(8,128)} %get-tuple-element.13), channel_id=1, source_target_pairs={{0,4},{1,5},{2,6},{3,7},{4,0},{5,1},{6,2},{7,3},{8,12},{9,13},{10,... | collective-permute-start | bytes 3538952 | tf_op jit(solution)/shard_map/ppermute | solution.py:97
  524.1 100.5 %collective-permute-start.16 = (f32[144,16,128]{2,1,0:T(8,128)}, f32[144,16,128]{2,1,0:T(8,128)S(1)}, u32[]{:S(2)}, u32[]{:S(2)}) collective-permute-start(f32[144,16,128]{2,1,0:T(8,128)} %get-tuple-element.12), channel_id=1, source_target_pairs={{0,5},{1,4},{2,7},{3,6},{4,1},{5,0},{6,3},{7,2},{8,13},{9,12},{10,... | collective-permute-start | bytes 3538952 | tf_op jit(solution)/shard_map/ppermute | solution.py:97
  526.5 99.2 %collective-permute-start.17 = (f32[144,16,128]{2,1,0:T(8,128)}, f32[144,16,128]{2,1,0:T(8,128)S(1)}, u32[]{:S(2)}, u32[]{:S(2)}) collective-permute-start(f32[144,16,128]{2,1,0:T(8,128)} %get-tuple-element.11), channel_id=1, source_target_pairs={{0,6},{1,7},{2,4},{3,5},{4,2},{5,3},{6,0},{7,1},{8,14},{9,15},{10,... | collective-permute-start | bytes 3538952 | tf_op jit(solution)/shard_map/ppermute | solution.py:97
  545.6 81.2 %collective-permute-start.18 = (f32[144,16,128]{2,1,0:T(8,128)}, f32[144,16,128]{2,1,0:T(8,128)S(1)}, u32[]{:S(2)}, u32[]{:S(2)}) collective-permute-start(f32[144,16,128]{2,1,0:T(8,128)} %get-tuple-element.10), channel_id=1, source_target_pairs={{0,7},{1,6},{2,5},{3,4},{4,3},{5,2},{6,1},{7,0},{8,15},{9,14},{10,... | collective-permute-start | bytes 3538952 | tf_op jit(solution)/shard_map/ppermute | solution.py:97
  627.9 8.5 %copy-start.9 = (f32[8,144]{1,0:T(8,128)S(1)}, f32[8,144]{1,0:T(8,128)}, u32[]{:S(2)}) copy-start(f32[8,144]{1,0:T(8,128)} %mul.415) | copy-start | bytes 13828
  627.9 14.5 %copy-start.15 = (f32[2048]{0:T(1024)S(1)}, f32[2048]{0:T(1024)}, u32[]{:S(2)}) copy-start(f32[2048]{0:T(1024)} %get-tuple-element.42) | copy-start | bytes 24580
  636.4 6.4 copy-start.11
  (6 other events, 37.4 us)
